TPU v7x, 512 devices: a whole 4x8x8 slice. The times are simulated.
512 devices in a mesh: dp: 8 (over y), ctx: 64 (over z, x, core).
Axes of the slice: x: 4, y: 8, z: 8, core: 2. Of those that a mesh axis runs over, the one named last changes fastest.
Arguments:
- queries: bfloat16 [8, 8192, 1024], P('dp', 'ctx'), may hold values from -6 to 6
- keys: bfloat16 [8, 8192, 1024], P('dp', 'ctx'), may hold values from -0.5390625 to 0.5390625
- values: bfloat16 [8, 8192, 1024], P('dp', 'ctx'), may hold values from -6 to 6
- gain: float32 [1024], replicated, may hold values from 0.1 to 1.9
- grad_out: bfloat16 [8, 8192, 1024], P('dp', 'ctx'), may hold values from -16 to 16
Outputs:
- output: bfloat16 [8, 8192, 1024], P('dp', 'ctx')
- grad_queries: bfloat16 [8, 8192, 1024], P('dp', 'ctx')
- grad_keys: bfloat16 [8, 8192, 1024], P('dp', 'ctx')
- grad_values: bfloat16 [8, 8192, 1024], P('dp', 'ctx')
- grad_gain: float32 [1024], replicated
All inputs are finite; a program needn't handle non-finite values.
Results may differ from a plain program's by a relative error of at most 0.006.
Values sent between devices are 32-bit elements; how exact they have to be, the bound alone decides.
No kernel may reach another device: no remote copies, remote signals or barrier semaphores. Data moves between devices by JAX's collectives and lax.ppermute only.
A program may use at most 128 MiB of HBM per device.

v0:
```python
import jax
import jax.numpy as jnp
from jax import lax
from jax.sharding import PartitionSpec as P

HEAD_DIM = 64
GROUP = 128


def entering(part, axis, combine, identity):
    place = lax.axis_index(axis)
    gathered = lax.all_gather(part, axis)
    state = jnp.zeros_like(part) + jnp.asarray(identity, part.dtype)

    def one(hop, state):
        return combine(state, lax.dynamic_index_in_dim(gathered, hop, 0, False))

    return lax.fori_loop(0, place, one, state)


def add_states(earlier, later_one):
    return earlier + later_one


def per_device(queries, keys, values, gain, grad_out):
    rows = queries.shape[1]
    width = queries.shape[2]
    heads = width // HEAD_DIM
    blocks = rows // GROUP
    shape4 = (blocks, GROUP, heads, HEAD_DIM)
    query_rows = queries.reshape(shape4)
    key_rows = keys.reshape(shape4)
    value_rows = values.reshape(shape4)
    f32 = jnp.float32
    block_kv = jnp.einsum("nrhd,nrhe->nhde", key_rows, value_rows, preferred_element_type=f32)
    local_kv = jnp.sum(block_kv, 0)
    empty_state = jnp.zeros((heads, HEAD_DIM, HEAD_DIM), f32)
    carried = entering(local_kv, "ctx", add_states, empty_state)
    state = carried[None] + (jnp.cumsum(block_kv, 0) - block_kv)
    state_low = state.astype(jnp.bfloat16)
    causal = jnp.tril(jnp.ones((GROUP, GROUP), bool))
    scores = jnp.where(
        causal[None, None],
        jnp.einsum("nthd,nshd->nhts", query_rows, key_rows, preferred_element_type=f32),
        0.0,
    ).astype(jnp.bfloat16)
    attn = jnp.einsum("nhts,nshe->nthe", scores, value_rows, preferred_element_type=f32)
    attn = attn + jnp.einsum("nthd,nhde->nthe", query_rows, state_low, preferred_element_type=f32)
    attn = attn.reshape(rows, width)
    inverse_rms = lax.rsqrt(jnp.mean(attn * attn, -1, keepdims=True) + 1e-06)
    normed = attn * inverse_rms
    output = (normed * gain).astype(jnp.bfloat16)
    grad_f = grad_out[0].astype(f32)
    gain_part = jnp.sum(grad_f * normed, 0)
    grad_norm = grad_f * gain
    grad_attn = (
        inverse_rms * (grad_norm - normed * jnp.mean(grad_norm * normed, -1, keepdims=True))
    ).astype(jnp.bfloat16)
    grad_attn = grad_attn.reshape(shape4)
    block_adjoint = jnp.einsum("nthd,nthe->nhde", query_rows, grad_attn, preferred_element_type=f32)
    local_adjoint = jnp.sum(block_adjoint, 0)
    dscores = jnp.where(
        causal[None, None],
        jnp.einsum("nthe,nshe->nhts", grad_attn, value_rows, preferred_element_type=f32),
        0.0,
    ).astype(jnp.bfloat16)
    grad_queries = jnp.einsum("nhts,nshd->nthd", dscores, key_rows, preferred_element_type=f32)
    grad_queries = grad_queries + jnp.einsum(
        "nthe,nhde->nthd", grad_attn, state_low, preferred_element_type=f32
    )
    grad_keys = jnp.einsum("nhts,nthd->nshd", dscores, query_rows, preferred_element_type=f32)
    grad_values = jnp.einsum("nhts,nthe->nshe", scores, grad_attn, preferred_element_type=f32)
    total, gain_ctx = lax.psum((local_adjoint, gain_part), "ctx")
    before = entering(local_adjoint, "ctx", add_states, empty_state)
    from_later = total - before - local_adjoint
    grad_gain = lax.psum(gain_ctx, "dp")
    from_end = jnp.cumsum(block_adjoint[::-1], 0)[::-1]
    later = from_later[None] + (from_end - block_adjoint)
    later_low = later.astype(jnp.bfloat16)
    grad_keys = grad_keys + jnp.einsum(
        "nshe,nhde->nshd", value_rows, later_low, preferred_element_type=f32
    )
    grad_values = grad_values + jnp.einsum(
        "nshd,nhde->nshe", key_rows, later_low, preferred_element_type=f32
    )
    flat = (1, rows, width)
    return (
        output.reshape(flat),
        grad_queries.reshape(flat).astype(jnp.bfloat16),
        grad_keys.reshape(flat).astype(jnp.bfloat16),
        grad_values.reshape(flat).astype(jnp.bfloat16),
        grad_gain,
    )


def solution(mesh):
    return jax.shard_map(
        per_device,
        mesh=mesh,
        in_specs=(
            P("dp", "ctx", None),
            P("dp", "ctx", None),
            P("dp", "ctx", None),
            P(),
            P("dp", "ctx", None),
        ),
        out_specs=(
            P("dp", "ctx", None),
            P("dp", "ctx", None),
            P("dp", "ctx", None),
            P("dp", "ctx", None),
            P(),
        ),
        check_vma=False,
    )
```

profile of v0, /device:TPU:8, one launch (start us, length us, event | category | flops | bytes accessed | tf_op | source)
XLA Modules:
  0.0 591.7 jit_solution(8018616743634753172)
XLA Ops:
  7.2 0.0 all-gather.5.cloned.1.call-start
  7.2 1.1 copy.48
  8.3 1.1 copy.49
  9.5 1.1 fusion.22
  10.5 0.0 all-gather.5.cloned.1.call-update
  10.6 0.0 all-gather.7.cloned.1.call-start
  10.6 0.8 mul.110
  11.4 1.1 copy.47
  12.5 1.1 copy.52
  13.6 0.4 fusion
  14.0 0.4 convolution_bitcast_fusion.3
  14.4 150.3 %all-gather.5.cloned.1.call-done = f32[1024,64,64]{2,1,0:T(8,128)} async-done(((f32[16,64,64]{2,1,0:T(8,128)}), f32[1024,64,64]{2,1,0:T(8,128)}) %all-gather.5.cloned.1.call-update) | async-done | bytes 16777232 | tf_op jit(solution)/shard_map/all_gather | solution.py:12
  164.7 1.1 add_convert_fusion.1
  165.9 0.3 fusion.16
  166.2 0.2 copy.53
  166.4 1.2 fusion.11
  167.6 0.3 convolution_bitcast_fusion.1
  168.0 0.0 copy-start
  168.0 1.0 copy.55
  169.0 0.0 all-gather.7.cloned.1.call-update
  169.0 0.0 all-reduce.2.cloned.1.call-start
  169.1 1.0 copy.51
  170.1 0.2 fusion.17
  170.3 0.4 fusion.1
  170.6 0.4 convolution_bitcast_fusion.2
  171.1 0.9 fusion.2
  172.0 1.8 copy.58
  173.8 203.0 %psum.22 = f32[1024]{0:T(1024)S(1)} all-reduce(f32[1024]{0:T(1024)S(1)} %get-tuple-element.76), channel_id=1, replica_groups=mesh['dp'=8,'ctx'=64] {'ctx'}, use_global_device_ids=true, to_apply=%region_8.9 | all-reduce | flops 1024 | bytes 8192 | tf_op jit(solution)/shard_map/psum | solution.py:73
  376.8 16.3 %psum.23 = f32[1024]{0:T(1024)} all-reduce(f32[1024]{0:T(1024)S(1)} %psum.22), channel_id=1, replica_groups=mesh['dp'=8,'ctx'=64] {'dp'}, use_global_device_ids=true, to_apply=%region_9.10 | all-reduce | flops 1024 | bytes 8192 | tf_op jit(solution)/shard_map/psum | solution.py:76
  393.1 1.9 multiply_convert_fusion
  395.0 0.3 fusion.23
  395.3 0.3 convolution_bitcast_fusion
  395.5 0.0 copy-done
  395.6 0.0 all-reduce.2.cloned.1.call-update
  395.6 0.0 all-gather.7.cloned.1.call-done
  395.7 0.2 copy.56
  395.9 185.8 %all-reduce.2.cloned.1.call-done = f32[16,64,64]{1,2,0:T(8,128)} async-done(((f32[16,64,64]{1,2,0:T(8,128)}), f32[16,64,64]{1,2,0:T(8,128)}) %all-reduce.2.cloned.1.call-update) | async-done | bytes 262160 | tf_op jit(solution)/shard_map/psum | solution.py:73
  581.6 1.3 add_convert_fusion
  583.0 0.2 fusion.4
  583.2 0.3 fusion.3
  583.5 0.8 copy.59
  584.3 0.8 copy.60
  (7 shorter events, 0.1 us)
Async XLA Ops:
  7.2 157.5 %all-gather.5.cloned.1.call-start = ((), (), s32[]{:S(2)}) async-start(), calls=%async_computation.1 | async-start | bytes 34078720 | tf_op jit(solution)/shard_map/all_gather | solution.py:12
  10.6 385.0 %all-gather.7.cloned.1.call-start = ((), (), s32[]{:S(2)}) async-start(), calls=%async_computation.2 | async-start | bytes 34078720 | tf_op jit(solution)/shard_map/all_gather | solution.py:12
  168.0 227.6 %copy-start = (f32[16,64,64]{1,2,0:T(8,128)}, f32[16,64,64]{1,2,0:T(8,128)S(1)}, u32[]{:S(2)}) copy-start(f32[16,64,64]{1,2,0:T(8,128)S(1)} %convolution_bitcast_fusion.1) | copy-start | bytes 786436
  169.0 412.6 %all-reduce.2.cloned.1.call-start = ((), (), s32[]{:S(2)}) async-start(), calls=%async_computation | async-start | bytes 1048576 | tf_op jit(solution)/shard_map/psum | solution.py:73
Sparse Core Ops, SparseCore 0:
  11.4 153.2 all-gather.4
  169.1 219.1 all-gather.6
  395.7 185.8 all-reduce.1
where the time goes:
time: 598 us; the launch traced here: 592 us
  waiting for transfers between devices  336 us (56%)
  blocking collectives  219 us (37%)
  between operations  13.9 us (2%)
  local copies, waits for them, and re-layouts  11.2 us (2%)
    psum x1, blocking collectives, per_device(): total, gain_ctx = lax.psum((local_adjoint, gain_part), 'ctx')  203 us
    psum x1, waiting for transfers between devices, per_device(): total, gain_ctx = lax.psum((local_adjoint, gain_part), 'ctx')  186 us
    all_gather x2, waiting for transfers between devices, entering(): gathered = lax.all_gather(part, axis)  150 us
    psum x1, blocking collectives, per_device(): grad_gain = lax.psum(gain_ctx, 'dp')  16.3 us
  transfers between devices with their start and end apart: 3, of which 2 were waited for; matrix products, arithmetic and copies ran while one was open for 2% of the time, Pallas kernels for 0%

commit v1 on v0

--- a/solution.py
+++ b/solution.py
@@ -2,6 +2,7 @@
 import jax.numpy as jnp
 from jax import lax
 from jax.sharding import PartitionSpec as P
+from jax.lax import axis_size, ppermute
 
 HEAD_DIM = 64
 GROUP = 128
@@ -73,7 +74,11 @@
     total, gain_ctx = lax.psum((local_adjoint, gain_part), "ctx")
     before = entering(local_adjoint, "ctx", add_states, empty_state)
     from_later = total - before - local_adjoint
-    grad_gain = lax.psum(gain_ctx, "dp")
+    nodes = axis_size("dp")
+    grad_gain = gain_ctx
+    for at in [[(c, c ^ no) for c in range(nodes)] for no in (1, 2, 4, 8, 16) if no < nodes]:
+        s_next = ppermute(grad_gain, "dp", at)
+        grad_gain = grad_gain + s_next
     from_end = jnp.cumsum(block_adjoint[::-1], 0)[::-1]
     later = from_later[None] + (from_end - block_adjoint)
     later_low = later.astype(jnp.bfloat16)

time: 598 us -> 600 us (level)
  blocking collectives: 219 us -> 203 us
  starting transfers between devices: 0.12 us -> 13.6 us
    psum x1 -> x0, blocking collectives: 16.3 us -> none  [per_device(): grad_gain = lax.psum(gain_ctx, 'dp')]
    ppermute x0 -> x3, starting transfers between devices: none -> 13.4 us  [per_device(): s_next = ppermute(grad_gain, 'dp', at)]
  transfers between devices with their start and end apart: 3 -> 6, of which waited for: 2 -> 5; matrix products, arithmetic and copies ran while one was open for 2% -> 2% of each run, Pallas kernels for 0% -> 0%
where the time goes in v1:
time: 600 us; the launch traced here: 593 us
  waiting for transfers between devices  339 us (56%)
  blocking collectives  203 us (34%)
  between operations  13.9 us (2%)
  starting transfers between devices  13.6 us (2%)
  local copies, waits for them, and re-layouts  9.43 us (2%)
  matrix products  8.31 us (1%)
    psum x1, blocking collectives, per_device(): total, gain_ctx = lax.psum((local_adjoint, gain_part), 'ctx')  203 us
    psum x1, waiting for transfers between devices, per_device(): total, gain_ctx = lax.psum((local_adjoint, gain_part), 'ctx')  187 us
    all_gather x2, waiting for transfers between devices, entering(): gathered = lax.all_gather(part, axis)  149 us
    ppermute x3, starting transfers between devices, per_device(): s_next = ppermute(grad_gain, 'dp', at)  13.4 us
  transfers between devices with their start and end apart: 6, of which 5 were waited for; matrix products, arithmetic and copies ran while one was open for 2% of the time, Pallas kernels for 0%

profile of v1, /device:TPU:8, one launch (start us, length us, event | category | flops | bytes accessed | tf_op | source)
XLA Modules:
  0.0 593.4 jit_solution(17233709543423744756)
XLA Ops:
  7.2 0.0 all-gather.5.cloned.1.call-start
  7.2 1.1 copy.48
  8.3 1.1 copy.49
  9.5 1.1 fusion.22
  10.5 0.0 all-gather.5.cloned.1.call-update
  10.6 0.0 all-gather.7.cloned.1.call-start
  10.6 0.8 mul.110
  11.4 1.1 copy.47
  12.5 1.1 copy.52
  13.6 0.4 fusion
  14.0 1.3 convolution_bitcast_fusion.3
  15.2 149.4 %all-gather.5.cloned.1.call-done = f32[1024,64,64]{2,1,0:T(8,128)} async-done(((f32[16,64,64]{2,1,0:T(8,128)}), f32[1024,64,64]{2,1,0:T(8,128)}) %all-gather.5.cloned.1.call-update) | async-done | bytes 16777232 | tf_op jit(solution)/shard_map/all_gather | solution.py:13
  164.7 1.1 add_convert_fusion.1
  165.9 1.4 fusion.16
  167.3 0.2 copy.53
  167.5 1.2 fusion.11
  168.7 0.3 convolution_bitcast_fusion.1
  169.0 0.0 copy-start
  169.0 1.0 copy.55
  170.0 0.0 all-gather.7.cloned.1.call-update
  170.1 0.0 all-reduce.2.cloned.1.call-start
  170.1 203.2 %psum.15 = f32[1024]{0:T(1024)S(1)} all-reduce(f32[1024]{0:T(1024)S(1)} %get-tuple-element.76), channel_id=1, replica_groups=mesh['dp'=8,'ctx'=64] {'ctx'}, use_global_device_ids=true, to_apply=%region_8.9 | all-reduce | flops 1024 | bytes 8192 | tf_op jit(solution)/shard_map/psum | solution.py:74
  373.3 2.4 collective-permute-start
  375.7 0.2 fusion.17
  375.9 0.4 fusion.1
  376.3 1.1 fusion.23
  377.4 0.3 convolution_bitcast_fusion
  377.6 0.5 convolution_bitcast_fusion.2
  378.1 0.7 collective-permute-done
  378.8 4.3 collective-permute-start.1
  383.1 0.2 fusion.2
  383.3 0.2 copy.51
  383.5 1.6 collective-permute-done.1
  385.1 6.7 %collective-permute-start.2 = (f32[1024]{0:T(1024)S(1)}, f32[1024]{0:T(1024)S(1)}, u32[]{:S(2)}, u32[]{:S(2)}) collective-permute-start(f32[1024]{0:T(1024)S(1)} %add.90), channel_id=1, source_target_pairs={{0,256},{64,320},{128,384},{192,448},{256,0},{320,64},{384,128},{4... | collective-permute-start | bytes 12296 | tf_op jit(solution)/shard_map/ppermute | solution.py:80
  391.9 1.5 multiply_convert_fusion
  393.4 0.8 copy.58
  394.2 0.0 copy-done
  394.2 0.0 all-reduce.2.cloned.1.call-update
  394.2 0.3 collective-permute-done.2
  394.5 0.6 add.91
  395.1 0.0 all-gather.7.cloned.1.call-done
  395.2 0.2 copy.56
  395.4 186.9 %all-reduce.2.cloned.1.call-done = f32[16,64,64]{1,2,0:T(8,128)} async-done(((f32[16,64,64]{1,2,0:T(8,128)}), f32[16,64,64]{1,2,0:T(8,128)}) %all-reduce.2.cloned.1.call-update) | async-done | bytes 262160 | tf_op jit(solution)/shard_map/psum | solution.py:74
  582.3 1.3 add_convert_fusion
  583.6 1.3 fusion.4
  584.9 0.3 fusion.3
  585.1 0.8 copy.59
  586.0 0.8 copy.60
  (9 shorter events, 0.1 us)
Async XLA Ops:
  7.2 157.5 %all-gather.5.cloned.1.call-start = ((), (), s32[]{:S(2)}) async-start(), calls=%async_computation.1 | async-start | bytes 34078720 | tf_op jit(solution)/shard_map/all_gather | solution.py:13
  10.6 384.6 %all-gather.7.cloned.1.call-start = ((), (), s32[]{:S(2)}) async-start(), calls=%async_computation.2 | async-start | bytes 34078720 | tf_op jit(solution)/shard_map/all_gather | solution.py:13
  169.0 225.2 %copy-start = (f32[16,64,64]{1,2,0:T(8,128)}, f32[16,64,64]{1,2,0:T(8,128)S(1)}, u32[]{:S(2)}) copy-start(f32[16,64,64]{1,2,0:T(8,128)S(1)} %convolution_bitcast_fusion.1) | copy-start | bytes 786436
  170.1 412.2 %all-reduce.2.cloned.1.call-start = ((), (), s32[]{:S(2)}) async-start(), calls=%async_computation | async-start | bytes 1048576 | tf_op jit(solution)/shard_map/psum | solution.py:74
  373.3 5.5 collective-permute-start
  378.8 6.4 %collective-permute-start.1 = (f32[1024]{0:T(1024)S(1)}, f32[1024]{0:T(1024)S(1)}, u32[]{:S(2)}, u32[]{:S(2)}) collective-permute-start(f32[1024]{0:T(1024)S(1)} %add.89), channel_id=1, source_target_pairs={{0,128},{64,192},{128,0},{192,64},{256,384},{320,448},{384,256},{4... | collective-permute-start | bytes 12296 | tf_op jit(solution)/shard_map/ppermute | solution.py:80
  385.1 9.4 %collective-permute-start.2 = (f32[1024]{0:T(1024)S(1)}, f32[1024]{0:T(1024)S(1)}, u32[]{:S(2)}, u32[]{:S(2)}) collective-permute-start(f32[1024]{0:T(1024)S(1)} %add.90), channel_id=1, source_target_pairs={{0,256},{64,320},{128,384},{192,448},{256,0},{320,64},{384,128},{4... | collective-permute-start | bytes 12296 | tf_op jit(solution)/shard_map/ppermute | solution.py:80
Sparse Core Ops, SparseCore 0:
  11.4 153.2 all-gather.4
  170.2 219.0 all-gather.6
  394.4 187.8 all-reduce.1
